TPU v7x, 256 devices: a whole 4x4x8 slice. The times are simulated.
256 devices in a mesh: leaf: 64 (over y, z, core), front: 4 (over x).
Axes of the slice: x: 4, y: 4, z: 8, core: 2. Of those that a mesh axis runs over, the one named last changes fastest.
Arguments:
- rhs_sub: float32 [8, 524288], P(None, ('leaf', 'front')), may hold values from -6 to 6
- rhs_sep: float32 [8, 16384], P(None, 'leaf'), may hold values from -6 to 6
- live_rows: int32 [256], P(('leaf', 'front')), may hold values from 256 to 2048, as said below
- lower_inv: bfloat16 [2048, 256, 256], P(('leaf', 'front')), as said below
- upper_inv: bfloat16 [2048, 256, 256], P(('leaf', 'front'))
- couple_low: bfloat16 [16384, 16384], P(('leaf', 'front')), may hold values from -0.1875 to 0.1875
- couple_up: bfloat16 [16384, 16384], P(('leaf', 'front')), may hold values from -0.046875 to 0.046875
- sep_lower_inv: bfloat16 [16384, 16384], P('leaf', 'front')
- sep_upper_inv: bfloat16 [16384, 16384], P('leaf', 'front')
- basis_sub: float32 [48, 524288], P(None, ('leaf', 'front')), may hold values from -0.0078125 to 0.0078125
- basis_sep: float32 [48, 16384], P(None, 'leaf'), may hold values from -0.0078125 to 0.0078125
Outputs:
- orth_sub: float32 [8, 524288], P(None, ('leaf', 'front'))
- orth_sep: float32 [8, 16384], P(None, 'leaf')
- coef: float32 [48, 8], replicated
Inputs may be any that keep to these rules, and one draw needn't show every extreme that they name: `live_rows`: each entry is a multiple of 256; some device has all 2048 rows live. Every block of lower_inv is lower triangular, and every block of upper_inv, sep_lower_inv and sep_upper_inv upper triangular, each with a diagonal between 1 and 1.5.
All inputs are finite; a program needn't handle non-finite values.
Results may differ from a plain program's by a relative error of at most 0.0055.
Values may be sent and summed in bfloat16 or wider, within the bound.
No kernel may reach another device: no remote copies, remote signals or barrier semaphores. Data moves between devices by JAX's collectives and lax.ppermute only.
A program may use at most 64 MiB of HBM per device.

v0:
```python
import jax
import jax.numpy as jnp
from jax import lax
from jax.sharding import Mesh, PartitionSpec as P


HIGH = lax.Precision.HIGHEST
F32 = jnp.float32
BF16 = jnp.bfloat16
BY_LAST = (((1,), (1,)), ((), ()))


def swap_core(value):
    return lax.ppermute(value, "c", [(0, 1), (1, 0)])


def sum_front(value):
    count = lax.axis_size("x")
    moved = [
        lax.ppermute(value, "x", [(i, (i + step) % count) for i in range(count)])
        for step in range(1, count)
    ]
    for other in moved:
        value = value + other
    return value


def exchange(value):
    return lax.all_to_all(value, ("y", "z"), 0, 0, tiled=True)


def spread(value, count):
    return jnp.broadcast_to(value[None], (count,) + value.shape)


def to_tiles(value, count):
    rows, cols = value.shape
    return value.reshape(rows, count, cols // count).transpose(1, 0, 2)


def from_tiles(value):
    count, rows, cols = value.shape
    return value.transpose(1, 0, 2).reshape(rows, count * cols)


def solve(
    rhs_sub,
    rhs_sep,
    live_rows,
    lower_inv,
    upper_inv,
    couple_low,
    couple_up,
    sep_lower_inv,
    sep_upper_inv,
    basis_sub,
    basis_sep,
):
    vecs, rows = rhs_sub.shape
    blocks, block, _ = lower_inv.shape
    border = couple_low.shape[0]
    basis = basis_sub.shape[0]
    own = rhs_sep.shape[1]
    group = lax.axis_size("y") * lax.axis_size("z")
    share = 1.0 / lax.axis_size("x")
    core = lax.axis_index("c")

    first = jnp.dot(rhs_sub[:, :block].astype(BF16), lower_inv[0], preferred_element_type=F32)
    border_rows = first[:, :border].astype(BF16)
    part = jnp.dot(border_rows, couple_low, preferred_element_type=F32)
    part = to_tiles(part, 2 * group).reshape(group, 2, vecs, own)
    keep = jnp.where(core == 0, part[:, 0], part[:, 1])
    send = jnp.where(core == 0, part[:, 1], part[:, 0]).astype(BF16)
    pack = (keep + swap_core(send).astype(F32)).astype(BF16)
    top_rhs = rhs_sep - sum_front(exchange(pack).astype(F32).sum(0))

    gram = lax.dot_general(basis_sub, basis_sub, BY_LAST, precision=HIGH)
    gram = gram + share * lax.dot_general(basis_sep, basis_sep, BY_LAST, precision=HIGH)
    gram = gram + swap_core(gram)
    high = gram.astype(BF16)
    low = (gram - high.astype(F32)).astype(BF16)
    lanes = sep_lower_inv.shape[1] // group
    gram = jnp.concatenate([high, low], axis=1)
    gram = jnp.pad(gram, ((0, group * vecs - basis), (0, lanes - 2 * basis)))
    gram = gram.reshape(group, vecs, lanes)
    mix = lax.dot_general(
        basis_sub[:, :block], upper_inv[0, :border].astype(F32), BY_LAST, precision=HIGH
    )

    live = lax.broadcasted_iota(jnp.int32, (1, blocks, 1), 1) * block < live_rows[0]
    shaped = lax.optimization_barrier(rhs_sub).astype(BF16).reshape(vecs, blocks, block)
    lower = jnp.einsum("vkr,krc->vkc", shaped, lower_inv, preferred_element_type=F32)
    lower = jnp.where(live, lower, 0.0)
    upper = jnp.einsum("vkr,krc->vkc", lower.astype(BF16), upper_inv, preferred_element_type=F32)
    upper = jnp.where(live, upper, 0.0).reshape(vecs, rows)
    coef = lax.dot_general(upper, basis_sub, BY_LAST, precision=HIGH)

    lower_part = jnp.dot(top_rhs.astype(BF16), sep_lower_inv, preferred_element_type=F32)
    lower_part = lower_part + swap_core(lower_part)
    mine = exchange(to_tiles(lower_part, group)).sum(0).astype(BF16)
    got = exchange(jnp.concatenate([spread(mine, group), gram], axis=1))
    gram = got[:, vecs:].astype(F32).sum(0)
    gram = gram[:, :basis] + gram[:, basis : 2 * basis]
    top_lower = from_tiles(got[:, :vecs])
    upper_part = lax.dot_general(top_lower, sep_upper_inv, BY_LAST, preferred_element_type=F32)
    got = sum_front(jnp.concatenate([upper_part, gram], axis=1))
    top_sol = got[:, :own]
    gram = got[:, own:]

    mine = exchange(spread(top_sol.astype(BF16), group))
    other = swap_core(mine)
    full = jnp.stack(
        [jnp.where(core == 0, mine, other), jnp.where(core == 0, other, mine)], axis=1
    )
    full = from_tiles(full.reshape(2 * group, vecs, own))
    correction = lax.dot_general(full, couple_up, BY_LAST, preferred_element_type=F32)

    coef = coef + share * lax.dot_general(top_sol, basis_sep, BY_LAST, precision=HIGH)
    coef = coef - lax.dot_general(correction, mix, BY_LAST, precision=HIGH)
    gap = jnp.zeros((vecs, lanes // 2 - basis), F32)
    coef = sum_front(coef + swap_core(coef))
    pack = jnp.concatenate([coef, gap, gram, gap], axis=1)
    got = exchange(spread(pack, group))
    coef = got[:, :, :basis].sum(0)
    gram = got[: basis // vecs, :, lanes // 2 : lanes // 2 + basis].reshape(basis, basis)

    updated = jnp.concatenate([first[:, :border] - correction, first[:, border:]], axis=1)
    head = jnp.dot(updated.astype(BF16), upper_inv[0], preferred_element_type=F32)
    upper_sol = jnp.concatenate([head, upper[:, block:]], axis=1)

    coef = 2.0 * coef - jnp.dot(coef, gram, precision=HIGH)
    orth_sub = upper_sol - jnp.dot(coef, basis_sub, precision=HIGH)
    orth_sep = top_sol - jnp.dot(coef, basis_sep, precision=HIGH)
    return (orth_sub, orth_sep, coef.T)


def solution(mesh):
    split = Mesh(mesh.devices.reshape(4, 8, 2, 4), ("y", "z", "c", "x"))
    leaf = ("y", "z", "c")
    every = ("y", "z", "c", "x")
    return jax.shard_map(
        solve,
        mesh=split,
        in_specs=(
            P(None, every),
            P(None, leaf),
            P(every),
            P(every, None, None),
            P(every, None, None),
            P(every, None),
            P(every, None),
            P(leaf, "x"),
            P(leaf, "x"),
            P(None, every),
            P(None, leaf),
        ),
        out_specs=(P(None, every), P(None, leaf), P()),
        check_vma=False,
    )
```

profile of v0, /device:TPU:2, one launch (start us, length us, event | category | flops | bytes accessed | tf_op | source)
XLA Modules:
  0.0 130.8 jit_solution(14196709030915737177)
XLA Ops:
  0.6 1.2 fusion.13
  3.0 1.3 %collective-permute-done = bf16[32,8,256]{2,1,0:T(8,128)(2,1)S(1)} collective-permute-done((bf16[32,8,256]{2,1,0:T(8,128)(2,1)S(1)}, bf16[32,8,256]{2,1,0:T(8,128)(2,1)S(1)}, u32[]{:S(2)}, u32[]{:S(2)}) %collective-permute-start) | collective-permute-done | bytes 131104 | tf_op jit(solution)/shard_map/ppermute | solution.py:14
  4.4 21.9 %all_to_all.25 = bf16[32,8,256]{2,1,0:T(8,128)(2,1)S(1)} all-to-all(bf16[32,8,256]{2,1,0:T(8,128)(2,1)S(1)} %fusion.6), channel_id=1, replica_groups=mesh['y'=4,'z'=8,'c'=2,'x'=4] {'y','z'}, dimensions={0} | all-to-all | bytes 262144 | tf_op jit(solution)/shard_map/all_to_all | solution.py:29
  26.4 1.6 %collective-permute-start.1 = (f32[8,256]{1,0:T(8,128)S(1)}, f32[8,256]{1,0:T(8,128)S(1)}, u32[]{:S(2)}, u32[]{:S(2)}) collective-permute-start(f32[8,256]{1,0:T(8,128)S(1)} %convert_reduce_fusion), channel_id=1, source_target_pairs={{0,1},{1,2},{2,3},{3,0},{4,5},{5,6},{6,7},{7,4},{8,9},{9,10},{10,1... | collective-permute-start | bytes 24584 | tf_op jit(solution)/shard_map/ppermute | solution.py:20
  27.9 1.1 collective-permute-start.2
  29.0 2.2 %collective-permute-start.3 = (f32[8,256]{1,0:T(8,128)S(1)}, f32[8,256]{1,0:T(8,128)S(1)}, u32[]{:S(2)}, u32[]{:S(2)}) collective-permute-start(f32[8,256]{1,0:T(8,128)S(1)} %convert_reduce_fusion), channel_id=1, source_target_pairs={{0,3},{1,0},{2,1},{3,2},{4,7},{5,4},{6,5},{7,6},{8,11},{9,8},{10,9... | collective-permute-start | bytes 24584 | tf_op jit(solution)/shard_map/ppermute | solution.py:20
  31.7 1.4 %collective-permute-done.2 = f32[8,256]{1,0:T(8,128)S(1)} collective-permute-done((f32[8,256]{1,0:T(8,128)S(1)}, f32[8,256]{1,0:T(8,128)S(1)}, u32[]{:S(2)}, u32[]{:S(2)}) %collective-permute-start.2) | collective-permute-done | bytes 8224 | tf_op jit(solution)/shard_map/ppermute | solution.py:20
  35.5 4.6 %all-to-all-start.1 = ((f32[32,8,128]{2,1,0:T(8,128)}), f32[32,8,128]{2,1,0:T(8,128)}, u32[]{:S(2)}, u32[]{:S(2)}) async-start(f32[32,8,128]{2,1,0:T(8,128)} %add_bitcast_fusion), calls=%async_computation.1 | async-start | bytes 262144 | tf_op jit(solution)/shard_map/all_to_all | solution.py:29
  41.6 9.4 %all-to-all-done.1 = f32[32,8,128]{2,1,0:T(8,128)} async-done(((f32[32,8,128]{2,1,0:T(8,128)}), f32[32,8,128]{2,1,0:T(8,128)}, u32[]{:S(2)}, u32[]{:S(2)}) %all-to-all-start.1) | async-done | bytes 131104 | tf_op jit(solution)/shard_map/all_to_all | solution.py:29
  51.9 1.5 %pad_maximum_fusion.1 = bf16[32,16,128]{2,1,0:T(8,128)(2,1)} fusion(bf16[32,8,128]{2,1,0:T(8,128)(2,1)} %fusion.20, bf16[32,8,128]{2,1,0:T(8,128)(2,1)S(1)} %broadcast_in_dim.41), kind=kLoop, calls=%fused_computation.26 | loop fusion | flops 262144 | bytes 262144 | tf_op jit(solution)/shard_map/concatenate | solution.py:101
  53.4 4.6 %all-to-all-start.2 = ((bf16[32,16,128]{2,1,0:T(8,128)(2,1)}), bf16[32,16,128]{2,1,0:T(8,128)(2,1)}, u32[]{:S(2)}, u32[]{:S(2)}) async-start(bf16[32,16,128]{2,1,0:T(8,128)(2,1)} %pad_maximum_fusion.1), calls=%async_computation.2 | async-start | bytes 262144 | tf_op jit(solution)/shard_map/all_to_all | solution.py:29
  58.0 1.4 %convert_element_type.70 = bf16[8,2048]{1,0:T(8,128)(2,1)} convert(f32[8,2048]{1,0:T(8,128)} %param.11) | non-fusion elementwise | flops 16384 | bytes 98304 | tf_op jit(solution)/shard_map/convert_element_type | solution.py:91
  60.6 7.7 %all-to-all-done.2 = bf16[32,16,128]{2,1,0:T(8,128)(2,1)} async-done(((bf16[32,16,128]{2,1,0:T(8,128)(2,1)}), bf16[32,16,128]{2,1,0:T(8,128)(2,1)}, u32[]{:S(2)}, u32[]{:S(2)}) %all-to-all-start.2) | async-done | bytes 131104 | tf_op jit(solution)/shard_map/all_to_all | solution.py:29
  69.3 2.3 %fusion.21 = f32[8,256]{1,0:T(8,128)S(1)} fusion(bf16[256,4096]{1,0:T(8,128)(2,1)} %param.19, bf16[32,16,128]{2,1,0:T(8,128)(2,1)} %all-to-all-done.2), kind=kOutput, calls=%fused_computation.42 | convolution fusion | flops 16777216 | bytes 2170880 | tf_op jit(solution)/shard_map/dot_general | solution.py:105
  72.2 1.2 collective-permute-start.6
  73.4 2.6 %collective-permute-start.7 = (f32[8,304]{1,0:T(8,128)S(1)}, f32[8,304]{1,0:T(8,128)}, u32[]{:S(2)}, u32[]{:S(2)}) collective-permute-start(f32[8,304]{1,0:T(8,128)S(1)} %pad_maximum_fusion.2), channel_id=1, source_target_pairs={{0,2},{1,3},{2,0},{3,1},{4,6},{5,7},{6,4},{7,5},{8,10},{9,11},{10,... | collective-permute-start | bytes 29192 | tf_op jit(solution)/shard_map/ppermute | solution.py:20
  76.0 2.0 %collective-permute-start.8 = (f32[8,304]{1,0:T(8,128)S(1)}, f32[8,304]{1,0:T(8,128)}, u32[]{:S(2)}, u32[]{:S(2)}) collective-permute-start(f32[8,304]{1,0:T(8,128)S(1)} %pad_maximum_fusion.2), channel_id=1, source_target_pairs={{0,3},{1,0},{2,1},{3,2},{4,7},{5,4},{6,5},{7,6},{8,11},{9,8},{10,9... | collective-permute-start | bytes 29192 | tf_op jit(solution)/shard_map/ppermute | solution.py:20
  78.1 2.3 %convolution_select_fusion = f32[8,8,256]{2,1,0:T(8,128)} fusion(bf16[8,256,256]{2,1,0:T(8,128)(2,1)S(1)} %copy-done.3, bf16[8,256,256]{2,1,0:T(8,128)(2,1)} %param.14, bf16[8,8,256]{2,0,1:T(8,128)(2,1)} %bitcast.101, pred[8]{0:T(512)(128)(4,1)} %multiply_compare_fusion), kind=kOutput, calls=%fused_computation.1 | convolution fusion | flops 16826368 | bytes 2195464 | tf_op jit(solution)/shard_map/vkr,krc->vkc/dot_general | solution.py:94
  81.8 4.6 %all-to-all-start.3 = ((bf16[32,8,256]{2,1,0:T(8,128)(2,1)}), bf16[32,8,256]{2,1,0:T(8,128)(2,1)}, u32[]{:S(2)}, u32[]{:S(2)}) async-start(bf16[32,8,256]{2,1,0:T(8,128)(2,1)} %broadcast_in_dim.42), calls=%async_computation.3 | async-start | bytes 262144 | tf_op jit(solution)/shard_map/all_to_all | solution.py:29
  87.1 1.2 fusion.37
  88.3 8.3 %all-to-all-done.3 = bf16[32,8,256]{2,1,0:T(8,128)(2,1)} async-done(((bf16[32,8,256]{2,1,0:T(8,128)(2,1)}), bf16[32,8,256]{2,1,0:T(8,128)(2,1)}, u32[]{:S(2)}, u32[]{:S(2)}) %all-to-all-start.3) | async-done | bytes 131104 | tf_op jit(solution)/shard_map/all_to_all | solution.py:29
  99.1 2.2 %subtract_convert_fusion.3 = (bf16[8,64]{1,0:T(8,128)(2,1)S(1)}, f32[8,64]{1,0:T(8,128)S(1)}) fusion(f32[8,256]{1,0:T(8,128)} %copy-done.7, bf16[8,16384]{1,0:T(8,128)(2,1)S(1)} %bitcast.98, bf16[64,16384]{1,0:T(8,128)(2,1)} %param.17), kind=kOutput, calls=%fused_computation.65 | convolution fusion | flops 16778240 | bytes 2364416 | tf_op jit(solution)/shard_map/dot_general | solution.py:116
  101.7 1.0 collective-permute-done.10
  102.7 1.0 collective-permute-start.11
  103.7 2.6 %collective-permute-start.12 = (f32[8,48]{1,0:T(8,128)S(1)}, f32[8,48]{1,0:T(8,128)S(1)}, u32[]{:S(2)}, u32[]{:S(2)}) collective-permute-start(f32[8,48]{1,0:T(8,128)S(1)} %add.62), channel_id=1, source_target_pairs={{0,2},{1,3},{2,0},{3,1},{4,6},{5,7},{6,4},{7,5},{8,10},{9,11},{10,... | collective-permute-start | bytes 4616 | tf_op jit(solution)/shard_map/ppermute | solution.py:20
  107.0 1.8 %collective-permute-done.12 = f32[8,48]{1,0:T(8,128)S(1)} collective-permute-done((f32[8,48]{1,0:T(8,128)S(1)}, f32[8,48]{1,0:T(8,128)S(1)}, u32[]{:S(2)}, u32[]{:S(2)}) %collective-permute-start.12) | collective-permute-done | bytes 1568 | tf_op jit(solution)/shard_map/ppermute | solution.py:20
  108.8 1.1 collective-permute-done.13
  110.7 4.6 %all-to-all-start.4 = ((f32[32,8,128]{2,1,0:T(8,128)}), f32[32,8,128]{2,1,0:T(8,128)}, u32[]{:S(2)}, u32[]{:S(2)}) async-start(f32[32,8,128]{2,1,0:T(8,128)} %broadcast_in_dim.48), calls=%async_computation.4 | async-start | bytes 262144 | tf_op jit(solution)/shard_map/all_to_all | solution.py:29
  116.0 1.4 %slice.85 = f32[8,1792]{1,0:T(8,128)} slice(f32[8,2048]{1,0:T(8,128)} %bitcast.100), slice={[0:8], [256:2048]} | slice | bytes 114688 | tf_op jit(solution)/shard_map/slice | solution.py:129
  118.2 7.4 %all-to-all-done.4 = f32[32,8,128]{2,1,0:T(8,128)} async-done(((f32[32,8,128]{2,1,0:T(8,128)}), f32[32,8,128]{2,1,0:T(8,128)}, u32[]{:S(2)}, u32[]{:S(2)}) %all-to-all-start.4) | async-done | bytes 131104 | tf_op jit(solution)/shard_map/all_to_all | solution.py:29
  127.5 1.6 %convolution_subtract_fusion.1 = f32[8,256]{1,0:T(8,128)} fusion(f32[8,48]{1,0:T(8,128)S(1)} %convolution_subtract_fusion.2, f32[48,256]{1,0:T(8,128)} %param.21, f32[8,304]{1,0:T(8,128)S(1)} %add_add_fusion), kind=kOutput, calls=%fused_computation.7 | convolution fusion | flops 1181696 | bytes 67072 | tf_op jit(solution)/shard_map/dot_general | solution.py:133
  129.1 1.8 %convolution_subtract_fusion = f32[8,2048]{1,0:T(8,128)} fusion(f32[8,48]{1,0:T(8,128)S(1)} %convolution_subtract_fusion.2, f32[48,2048]{1,0:T(8,128)S(1)} %copy-done.1, f32[8,1792]{1,0:T(8,128)} %slice.85, f32[8,256]{1,0:T(8,128)} %fusion.11), kind=kOutput, calls=%fused_computation | convolution fusion | flops 9469952 | bytes 525824 | tf_op jit(solution)/shard_map/dot_general | solution.py:132
  (69 shorter events, 18.5 us)
Async XLA Ops:
  0.6 1.7 %copy-start = (bf16[64,16384]{1,0:T(8,128)(2,1)S(1)}, bf16[64,16384]{1,0:T(8,128)(2,1)}, u32[]{:S(2)}) copy-start(bf16[64,16384]{1,0:T(8,128)(2,1)} %param.16) | copy-start | bytes 6291460
  2.3 0.6 copy-start.7
  2.3 28.9 %copy-start.1 = (f32[48,2048]{1,0:T(8,128)S(1)}, f32[48,2048]{1,0:T(8,128)}, u32[]{:S(2)}) copy-start(f32[48,2048]{1,0:T(8,128)} %param.20) | copy-start | bytes 1179652
  2.3 30.8 %copy-start.9 = (f32[8,256]{1,0:T(8,128)S(1)}, f32[8,256]{1,0:T(8,128)}, u32[]{:S(2)}) copy-start(f32[8,256]{1,0:T(8,128)} %param.12) | copy-start | bytes 24580
  2.9 30.2 %copy-start.2 = (bf16[256,4096]{1,0:T(8,128)(2,1)S(1)}, bf16[256,4096]{1,0:T(8,128)(2,1)}, u32[]{:S(2)}) copy-start(bf16[256,4096]{1,0:T(8,128)(2,1)} %param.18) | copy-start | bytes 6291460
  2.9 30.6 %copy-start.4 = (f32[48,256]{1,0:T(8,128)S(1)}, f32[48,256]{1,0:T(8,128)}, u32[]{:S(2)}) copy-start(f32[48,256]{1,0:T(8,128)} %param.21) | copy-start | bytes 147460
  2.9 1.4 %collective-permute-start = (bf16[32,8,256]{2,1,0:T(8,128)(2,1)S(1)}, bf16[32,8,256]{2,1,0:T(8,128)(2,1)S(1)}, u32[]{:S(2)}, u32[]{:S(2)}) collective-permute-start(bf16[32,8,256]{2,1,0:T(8,128)(2,1)S(1)} %fusion.7), channel_id=1, source_target_pairs={{0,4},{4,0},{1,5},{5,1},{2,6},{6,2},{3,7},{7,3},{8,12},{12,8},{9,1... | collective-permute-start | bytes 393224 | tf_op jit(solution)/shard_map/ppermute | solution.py:14
  26.4 5.3 %collective-permute-start.1 = (f32[8,256]{1,0:T(8,128)S(1)}, f32[8,256]{1,0:T(8,128)S(1)}, u32[]{:S(2)}, u32[]{:S(2)}) collective-permute-start(f32[8,256]{1,0:T(8,128)S(1)} %convert_reduce_fusion), channel_id=1, source_target_pairs={{0,1},{1,2},{2,3},{3,0},{4,5},{5,6},{6,7},{7,4},{8,9},{9,10},{10,1... | collective-permute-start | bytes 24584 | tf_op jit(solution)/shard_map/ppermute | solution.py:20
  27.9 5.2 %collective-permute-start.2 = (f32[8,256]{1,0:T(8,128)S(1)}, f32[8,256]{1,0:T(8,128)S(1)}, u32[]{:S(2)}, u32[]{:S(2)}) collective-permute-start(f32[8,256]{1,0:T(8,128)S(1)} %convert_reduce_fusion), channel_id=1, source_target_pairs={{0,2},{1,3},{2,0},{3,1},{4,6},{5,7},{6,4},{7,5},{8,10},{9,11},{10,... | collective-permute-start | bytes 24584 | tf_op jit(solution)/shard_map/ppermute | solution.py:20
  29.0 4.0 %collective-permute-start.3 = (f32[8,256]{1,0:T(8,128)S(1)}, f32[8,256]{1,0:T(8,128)S(1)}, u32[]{:S(2)}, u32[]{:S(2)}) collective-permute-start(f32[8,256]{1,0:T(8,128)S(1)} %convert_reduce_fusion), channel_id=1, source_target_pairs={{0,3},{1,0},{2,1},{3,2},{4,7},{5,4},{6,5},{7,6},{8,11},{9,8},{10,9... | collective-permute-start | bytes 24584 | tf_op jit(solution)/shard_map/ppermute | solution.py:20
  33.5 44.6 %copy-start.3 = (bf16[8,256,256]{2,1,0:T(8,128)(2,1)S(1)}, bf16[8,256,256]{2,1,0:T(8,128)(2,1)}, u32[]{:S(2)}) copy-start(bf16[8,256,256]{2,1,0:T(8,128)(2,1)} %param.15) | copy-start | bytes 3145732
  33.5 1.4 %collective-permute-start.4 = (f32[8,4096]{1,0:T(8,128)S(1)}, f32[8,4096]{1,0:T(8,128)S(1)}, u32[]{:S(2)}, u32[]{:S(2)}) collective-permute-start(f32[8,4096]{1,0:T(8,128)S(1)} %fusion.29), channel_id=1, source_target_pairs={{0,4},{4,0},{1,5},{5,1},{2,6},{6,2},{3,7},{7,3},{8,12},{12,8},{9,1... | collective-permute-start | bytes 393224 | tf_op jit(solution)/shard_map/ppermute | solution.py:14
  34.3 5.8 %collective-permute-start.5 = (f32[48,48]{1,0:T(8,128)}, f32[48,48]{1,0:T(8,128)}, u32[]{:S(2)}, u32[]{:S(2)}) collective-permute-start(f32[48,48]{1,0:T(8,128)} %fusion.2), channel_id=1, source_target_pairs={{0,4},{4,0},{1,5},{5,1},{2,6},{6,2},{3,7},{7,3},{8,12},{12,8},{9,1... | collective-permute-start | bytes 27656 | tf_op jit(solution)/shard_map/ppermute | solution.py:14
  35.5 15.4 %all-to-all-start.1 = ((f32[32,8,128]{2,1,0:T(8,128)}), f32[32,8,128]{2,1,0:T(8,128)}, u32[]{:S(2)}, u32[]{:S(2)}) async-start(f32[32,8,128]{2,1,0:T(8,128)} %add_bitcast_fusion), calls=%async_computation.1 | async-start | bytes 262144 | tf_op jit(solution)/shard_map/all_to_all | solution.py:29
  53.4 14.9 %all-to-all-start.2 = ((bf16[32,16,128]{2,1,0:T(8,128)(2,1)}), bf16[32,16,128]{2,1,0:T(8,128)(2,1)}, u32[]{:S(2)}, u32[]{:S(2)}) async-start(bf16[32,16,128]{2,1,0:T(8,128)(2,1)} %pad_maximum_fusion.1), calls=%async_computation.2 | async-start | bytes 262144 | tf_op jit(solution)/shard_map/all_to_all | solution.py:29
  71.6 0.6 copy-start.6
  72.2 8.1 %collective-permute-start.6 = (f32[8,304]{1,0:T(8,128)S(1)}, f32[8,304]{1,0:T(8,128)}, u32[]{:S(2)}, u32[]{:S(2)}) collective-permute-start(f32[8,304]{1,0:T(8,128)S(1)} %pad_maximum_fusion.2), channel_id=1, source_target_pairs={{0,1},{1,2},{2,3},{3,0},{4,5},{5,6},{6,7},{7,4},{8,9},{9,10},{10,1... | collective-permute-start | bytes 29192 | tf_op jit(solution)/shard_map/ppermute | solution.py:20
  73.4 6.9 %collective-permute-start.7 = (f32[8,304]{1,0:T(8,128)S(1)}, f32[8,304]{1,0:T(8,128)}, u32[]{:S(2)}, u32[]{:S(2)}) collective-permute-start(f32[8,304]{1,0:T(8,128)S(1)} %pad_maximum_fusion.2), channel_id=1, source_target_pairs={{0,2},{1,3},{2,0},{3,1},{4,6},{5,7},{6,4},{7,5},{8,10},{9,11},{10,... | collective-permute-start | bytes 29192 | tf_op jit(solution)/shard_map/ppermute | solution.py:20
  76.0 4.3 %collective-permute-start.8 = (f32[8,304]{1,0:T(8,128)S(1)}, f32[8,304]{1,0:T(8,128)}, u32[]{:S(2)}, u32[]{:S(2)}) collective-permute-start(f32[8,304]{1,0:T(8,128)S(1)} %pad_maximum_fusion.2), channel_id=1, source_target_pairs={{0,3},{1,0},{2,1},{3,2},{4,7},{5,4},{6,5},{7,6},{8,11},{9,8},{10,9... | collective-permute-start | bytes 29192 | tf_op jit(solution)/shard_map/ppermute | solution.py:20
  81.8 14.8 %all-to-all-start.3 = ((bf16[32,8,256]{2,1,0:T(8,128)(2,1)}), bf16[32,8,256]{2,1,0:T(8,128)(2,1)}, u32[]{:S(2)}, u32[]{:S(2)}) async-start(bf16[32,8,256]{2,1,0:T(8,128)(2,1)} %broadcast_in_dim.42), calls=%async_computation.3 | async-start | bytes 262144 | tf_op jit(solution)/shard_map/all_to_all | solution.py:29
  96.6 4.8 %copy-start.5 = (f32[48,64]{1,0:T(8,128)S(1)}, f32[48,64]{1,0:T(8,128)}, u32[]{:S(2)}) copy-start(f32[48,64]{1,0:T(8,128)} %fusion.22) | copy-start | bytes 36868
  96.6 1.6 %collective-permute-start.9 = (bf16[32,8,256]{2,1,0:T(8,128)(2,1)}, bf16[32,8,256]{2,1,0:T(8,128)(2,1)S(1)}, u32[]{:S(2)}, u32[]{:S(2)}) collective-permute-start(bf16[32,8,256]{2,1,0:T(8,128)(2,1)} %all-to-all-done.3), channel_id=1, source_target_pairs={{0,4},{4,0},{1,5},{5,1},{2,6},{6,2},{3,7},{7,3},{8,12},{12,8},{9,1... | collective-permute-start | bytes 393224 | tf_op jit(solution)/shard_map/ppermute | solution.py:14
  101.5 1.2 collective-permute-start.10
  102.7 4.2 %collective-permute-start.11 = (f32[8,48]{1,0:T(8,128)S(1)}, f32[8,48]{1,0:T(8,128)S(1)}, u32[]{:S(2)}, u32[]{:S(2)}) collective-permute-start(f32[8,48]{1,0:T(8,128)S(1)} %add.62), channel_id=1, source_target_pairs={{0,1},{1,2},{2,3},{3,0},{4,5},{5,6},{6,7},{7,4},{8,9},{9,10},{10,1... | collective-permute-start | bytes 4616 | tf_op jit(solution)/shard_map/ppermute | solution.py:20
  103.7 5.1 %collective-permute-start.12 = (f32[8,48]{1,0:T(8,128)S(1)}, f32[8,48]{1,0:T(8,128)S(1)}, u32[]{:S(2)}, u32[]{:S(2)}) collective-permute-start(f32[8,48]{1,0:T(8,128)S(1)} %add.62), channel_id=1, source_target_pairs={{0,2},{1,3},{2,0},{3,1},{4,6},{5,7},{6,4},{7,5},{8,10},{9,11},{10,... | collective-permute-start | bytes 4616 | tf_op jit(solution)/shard_map/ppermute | solution.py:20
  106.3 3.6 %collective-permute-start.13 = (f32[8,48]{1,0:T(8,128)S(1)}, f32[8,48]{1,0:T(8,128)S(1)}, u32[]{:S(2)}, u32[]{:S(2)}) collective-permute-start(f32[8,48]{1,0:T(8,128)S(1)} %add.62), channel_id=1, source_target_pairs={{0,3},{1,0},{2,1},{3,2},{4,7},{5,4},{6,5},{7,6},{8,11},{9,8},{10,9... | collective-permute-start | bytes 4616 | tf_op jit(solution)/shard_map/ppermute | solution.py:20
  110.7 14.9 %all-to-all-start.4 = ((f32[32,8,128]{2,1,0:T(8,128)}), f32[32,8,128]{2,1,0:T(8,128)}, u32[]{:S(2)}, u32[]{:S(2)}) async-start(f32[32,8,128]{2,1,0:T(8,128)} %broadcast_in_dim.48), calls=%async_computation.4 | async-start | bytes 262144 | tf_op jit(solution)/shard_map/all_to_all | solution.py:29
  127.5 3.3 %copy-start.8 = (f32[8,48]{1,0:T(8,128)}, f32[8,48]{1,0:T(8,128)S(1)}, u32[]{:S(2)}) copy-start(f32[8,48]{1,0:T(8,128)S(1)} %convolution_subtract_fusion.2) | copy-start | bytes 4612
where the time goes:
time: 132 us; the launch traced here: 131 us
  waiting for transfers between devices  40.1 us (30%)
  starting transfers between devices  34 us (26%)
  blocking collectives  21.9 us (17%)
  matrix products  18.1 us (14%)
  other arithmetic  10.4 us (8%)
  local copies, waits for them, and re-layouts  4.87 us (4%)
  between operations  1.45 us (1%)
    all_to_all x4, waiting for transfers between devices, exchange(): return lax.all_to_all(value, ('y', 'z'), 0, 0, tiled=True)  32.7 us
    all_to_all x1, blocking collectives, exchange(): return lax.all_to_all(value, ('y', 'z'), 0, 0, tiled=True)  21.9 us
    all_to_all x4, starting transfers between devices, exchange(): return lax.all_to_all(value, ('y', 'z'), 0, 0, tiled=True)  18.3 us
    ppermute x9, starting transfers between devices, sum_front(): lax.ppermute(value, 'x', [(i, (i + step) % count) for i in range(count)])  14.9 us
    ppermute x9, waiting for transfers between devices, sum_front(): lax.ppermute(value, 'x', [(i, (i + step) % count) for i in range(count)])  4.39 us
    ppermute x5, waiting for transfers between devices, swap_core(): return lax.ppermute(value, 'c', [(0, 1), (1, 0)])  3.01 us
  transfers between devices with their start and end apart: 18, of which 10 were waited for; matrix products, arithmetic and copies ran while one was open for 10% of the time, Pallas kernels for 0%

commit v1 on v0

--- a/solution.py
+++ b/solution.py
@@ -1,6 +1,8 @@
 import jax
 import jax.numpy as jnp
 from jax import lax
+from jax.experimental import pallas as pl
+from jax.experimental.pallas import tpu as pltpu
 from jax.sharding import Mesh, PartitionSpec as P
 
 
@@ -41,6 +43,46 @@
 def from_tiles(value):
     count, rows, cols = value.shape
     return value.transpose(1, 0, 2).reshape(rows, count * cols)
+
+
+def finish_kernel(got_ref, upper_ref, head_ref, top_ref, sub_ref, sep_ref, *outs):
+    sub_out, sep_out, coef_out = outs
+    basis = sub_ref.shape[0]
+    vecs, own = head_ref.shape
+    middle = got_ref.shape[2] // 2
+    coef = got_ref[0]
+    for index in range(1, got_ref.shape[0]):
+        coef = coef + got_ref[index]
+    coef = coef[:, :basis]
+    gram = got_ref[: basis // vecs].reshape(basis, 2 * middle)[:, middle : middle + basis]
+    coef = 2.0 * coef - jnp.dot(coef, gram, precision=HIGH, preferred_element_type=F32)
+    coef_out[...] = coef
+    sep_out[...] = top_ref[:, :own] - jnp.dot(
+        coef, sep_ref[...], precision=HIGH, preferred_element_type=F32
+    )
+    moved = jnp.dot(coef, sub_ref[...], precision=HIGH, preferred_element_type=F32)
+    sub_out[:, :own] = head_ref[...] - moved[:, :own]
+    sub_out[:, own:] = upper_ref[:, own:] - moved[:, own:]
+
+
+def finish(got, upper, head, top_sol, basis_sub, basis_sep):
+    basis, rows = basis_sub.shape
+    vecs, own = head.shape
+    return pl.pallas_call(
+        finish_kernel,
+        out_shape=(
+            jax.ShapeDtypeStruct((vecs, rows), F32),
+            jax.ShapeDtypeStruct((vecs, own), F32),
+            jax.ShapeDtypeStruct((vecs, basis), F32),
+        ),
+        compiler_params=pltpu.CompilerParams(vmem_limit_bytes=8 << 20),
+        cost_estimate=pl.CostEstimate(
+            flops=2 * vecs * basis * rows,
+            bytes_accessed=4 * (basis_sub.size + 2 * upper.size),
+            transcendentals=0,
+        ),
+        name="finish",
+    )(got, upper, head, top_sol, basis_sub, basis_sep)
 
 
 def solve(
@@ -103,9 +145,9 @@
     gram = gram[:, :basis] + gram[:, basis : 2 * basis]
     top_lower = from_tiles(got[:, :vecs])
     upper_part = lax.dot_general(top_lower, sep_upper_inv, BY_LAST, preferred_element_type=F32)
-    got = sum_front(jnp.concatenate([upper_part, gram], axis=1))
-    top_sol = got[:, :own]
-    gram = got[:, own:]
+    top_all = sum_front(jnp.concatenate([upper_part, gram], axis=1))
+    top_sol = top_all[:, :own]
+    gram = top_all[:, own:]
 
     mine = exchange(spread(top_sol.astype(BF16), group))
     other = swap_core(mine)
@@ -121,16 +163,10 @@
     coef = sum_front(coef + swap_core(coef))
     pack = jnp.concatenate([coef, gap, gram, gap], axis=1)
     got = exchange(spread(pack, group))
-    coef = got[:, :, :basis].sum(0)
-    gram = got[: basis // vecs, :, lanes // 2 : lanes // 2 + basis].reshape(basis, basis)
-
     updated = jnp.concatenate([first[:, :border] - correction, first[:, border:]], axis=1)
     head = jnp.dot(updated.astype(BF16), upper_inv[0], preferred_element_type=F32)
-    upper_sol = jnp.concatenate([head, upper[:, block:]], axis=1)
 
-    coef = 2.0 * coef - jnp.dot(coef, gram, precision=HIGH)
-    orth_sub = upper_sol - jnp.dot(coef, basis_sub, precision=HIGH)
-    orth_sep = top_sol - jnp.dot(coef, basis_sep, precision=HIGH)
+    orth_sub, orth_sep, coef = finish(got, upper, head, top_all, basis_sub, basis_sep)
     return (orth_sub, orth_sep, coef.T)
 
 

time: 132 us -> 119 us (0.902)
  the two profiles are of different devices: /device:TPU:2 before, /device:TPU:0 now
where the time goes in v1:
time: 119 us; the launch traced here: 117 us
  waiting for transfers between devices  48.5 us (41%)
  starting transfers between devices  30.3 us (25%)
  blocking collectives  20.2 us (17%)
  matrix products  11.7 us (10%)
  local copies, waits for them, and re-layouts  1.9 us (2%)
  other arithmetic  1.86 us (2%)
  between operations  1.5 us (1%)
  Pallas kernels  1.19 us (1%)
    all_to_all x4, waiting for transfers between devices, exchange(): return lax.all_to_all(value, ('y', 'z'), 0, 0, tiled=True)  38.7 us
    all_to_all x1, blocking collectives, exchange(): return lax.all_to_all(value, ('y', 'z'), 0, 0, tiled=True)  20.2 us
    all_to_all x4, starting transfers between devices, exchange(): return lax.all_to_all(value, ('y', 'z'), 0, 0, tiled=True)  15.4 us
    ppermute x9, starting transfers between devices, sum_front(): lax.ppermute(value, 'x', [(i, (i + step) % count) for i in range(count)])  14.1 us
    ppermute x9, waiting for transfers between devices, sum_front(): lax.ppermute(value, 'x', [(i, (i + step) % count) for i in range(count)])  5.64 us
    ppermute x5, waiting for transfers between devices, swap_core(): return lax.ppermute(value, 'c', [(0, 1), (1, 0)])  4.13 us
  transfers between devices with their start and end apart: 18, of which 14 were waited for; matrix products, arithmetic and copies ran while one was open for 5% of the time, Pallas kernels for 0%

profile of v1, /device:TPU:0, one launch (start us, length us, event | category | flops | bytes accessed | tf_op | source)
XLA Modules:
  0.0 117.1 jit_solution(16186899971299370728)
XLA Ops:
  0.6 1.2 %fusion.13 = f32[8,256]{1,0:T(8,128)S(1)} fusion(bf16[8,256,256]{2,1,0:T(8,128)(2,1)} %param.14, f32[8,2048]{1,0:T(8,128)} %param.11), kind=kOutput, calls=%fused_computation.25 | convolution fusion | flops 1048576 | bytes 143360 | tf_op jit(solution)/shard_map/dot_general | solution.py:110
  2.8 1.3 %collective-permute-done = bf16[32,8,256]{2,1,0:T(8,128)(2,1)S(1)} collective-permute-done((bf16[32,8,256]{2,1,0:T(8,128)(2,1)S(1)}, bf16[32,8,256]{2,1,0:T(8,128)(2,1)S(1)}, u32[]{:S(2)}, u32[]{:S(2)}) %collective-permute-start) | collective-permute-done | bytes 131104 | tf_op jit(solution)/shard_map/ppermute | solution.py:16
  4.2 20.2 %all_to_all.25 = bf16[32,8,256]{2,1,0:T(8,128)(2,1)S(1)} all-to-all(bf16[32,8,256]{2,1,0:T(8,128)(2,1)S(1)} %fusion.6), channel_id=1, replica_groups=mesh['y'=4,'z'=8,'c'=2,'x'=4] {'y','z'}, dimensions={0} | all-to-all | bytes 262144 | tf_op jit(solution)/shard_map/all_to_all | solution.py:31
  24.5 1.6 %collective-permute-start.1 = (f32[8,256]{1,0:T(8,128)S(1)}, f32[8,256]{1,0:T(8,128)S(1)}, u32[]{:S(2)}, u32[]{:S(2)}) collective-permute-start(f32[8,256]{1,0:T(8,128)S(1)} %convert_reduce_fusion), channel_id=1, source_target_pairs={{0,1},{1,2},{2,3},{3,0},{4,5},{5,6},{6,7},{7,4},{8,9},{9,10},{10,1... | collective-permute-start | bytes 24584 | tf_op jit(solution)/shard_map/ppermute | solution.py:22
  26.0 2.7 %collective-permute-start.2 = (f32[8,256]{1,0:T(8,128)S(1)}, f32[8,256]{1,0:T(8,128)S(1)}, u32[]{:S(2)}, u32[]{:S(2)}) collective-permute-start(f32[8,256]{1,0:T(8,128)S(1)} %convert_reduce_fusion), channel_id=1, source_target_pairs={{0,2},{1,3},{2,0},{3,1},{4,6},{5,7},{6,4},{7,5},{8,10},{9,11},{10,... | collective-permute-start | bytes 24584 | tf_op jit(solution)/shard_map/ppermute | solution.py:22
  28.8 1.4 %collective-permute-start.3 = (f32[8,256]{1,0:T(8,128)S(1)}, f32[8,256]{1,0:T(8,128)S(1)}, u32[]{:S(2)}, u32[]{:S(2)}) collective-permute-start(f32[8,256]{1,0:T(8,128)S(1)} %convert_reduce_fusion), channel_id=1, source_target_pairs={{0,3},{1,0},{2,1},{3,2},{4,7},{5,4},{6,5},{7,6},{8,11},{9,8},{10,9... | collective-permute-start | bytes 24584 | tf_op jit(solution)/shard_map/ppermute | solution.py:22
  31.2 1.2 %collective-permute-done.3 = f32[8,256]{1,0:T(8,128)S(1)} collective-permute-done((f32[8,256]{1,0:T(8,128)S(1)}, f32[8,256]{1,0:T(8,128)S(1)}, u32[]{:S(2)}, u32[]{:S(2)}) %collective-permute-start.3) | collective-permute-done | bytes 8224 | tf_op jit(solution)/shard_map/ppermute | solution.py:22
  34.2 0.7 add_bitcast_fusion
  34.8 3.8 %all-to-all-start.1 = ((f32[32,8,128]{2,1,0:T(8,128)}), f32[32,8,128]{2,1,0:T(8,128)S(1)}, u32[]{:S(2)}, u32[]{:S(2)}) async-start(f32[32,8,128]{2,1,0:T(8,128)} %add_bitcast_fusion), calls=%async_computation.1 | async-start | bytes 262144 | tf_op jit(solution)/shard_map/all_to_all | solution.py:31
  38.8 10.8 %all-to-all-done.1 = f32[32,8,128]{2,1,0:T(8,128)S(1)} async-done(((f32[32,8,128]{2,1,0:T(8,128)}), f32[32,8,128]{2,1,0:T(8,128)S(1)}, u32[]{:S(2)}, u32[]{:S(2)}) %all-to-all-start.1) | async-done | bytes 131104 | tf_op jit(solution)/shard_map/all_to_all | solution.py:31
  49.6 0.7 pad_maximum_fusion.1
  50.3 3.8 %all-to-all-start.2 = ((bf16[32,16,128]{2,1,0:T(8,128)(2,1)}), bf16[32,16,128]{2,1,0:T(8,128)(2,1)S(1)}, u32[]{:S(2)}, u32[]{:S(2)}) async-start(bf16[32,16,128]{2,1,0:T(8,128)(2,1)} %pad_maximum_fusion.1), calls=%async_computation.2 | async-start | bytes 262144 | tf_op jit(solution)/shard_map/all_to_all | solution.py:31
  54.8 9.7 %all-to-all-done.2 = bf16[32,16,128]{2,1,0:T(8,128)(2,1)S(1)} async-done(((bf16[32,16,128]{2,1,0:T(8,128)(2,1)}), bf16[32,16,128]{2,1,0:T(8,128)(2,1)S(1)}, u32[]{:S(2)}, u32[]{:S(2)}) %all-to-all-start.2) | async-done | bytes 131104 | tf_op jit(solution)/shard_map/all_to_all | solution.py:31
  64.7 2.2 %fusion.21 = f32[8,256]{1,0:T(8,128)S(1)} fusion(bf16[256,4096]{1,0:T(8,128)(2,1)} %param.19, bf16[32,16,128]{2,1,0:T(8,128)(2,1)S(1)} %all-to-all-done.2), kind=kOutput, calls=%fused_computation.38 | convolution fusion | flops 16777216 | bytes 2170880 | tf_op jit(solution)/shard_map/dot_general | solution.py:147
  67.2 3.8 %collective-permute-start.7 = (f32[8,304]{1,0:T(8,128)S(1)}, f32[8,304]{1,0:T(8,128)S(1)}, u32[]{:S(2)}, u32[]{:S(2)}) collective-permute-start(f32[8,304]{1,0:T(8,128)S(1)} %pad_maximum_fusion.2), channel_id=1, source_target_pairs={{0,2},{1,3},{2,0},{3,1},{4,6},{5,7},{6,4},{7,5},{8,10},{9,11},{10,... | collective-permute-start | bytes 29192 | tf_op jit(solution)/shard_map/ppermute | solution.py:22
  71.1 1.9 %convolution_select_fusion = f32[8,8,256]{2,1,0:T(8,128)S(1)} fusion(bf16[8,256,256]{2,1,0:T(8,128)(2,1)} %param.15, bf16[8,256,256]{2,1,0:T(8,128)(2,1)} %param.14, bf16[8,8,256]{2,0,1:T(8,128)(2,1)S(1)} %bitcast.93, pred[8]{0:T(512)(128)(4,1)S(1)} %multiply_compare_fusion), kind=kOutput, calls=%fused_computation | convolution fusion | flops 16826368 | bytes 2195464 | tf_op jit(solution)/shard_map/vkr,krc->vkc/dot_general | solution.py:136
  73.0 1.7 %collective-permute-done.8 = f32[8,304]{1,0:T(8,128)S(1)} collective-permute-done((f32[8,304]{1,0:T(8,128)S(1)}, f32[8,304]{1,0:T(8,128)S(1)}, u32[]{:S(2)}, u32[]{:S(2)}) %collective-permute-start.8) | collective-permute-done | bytes 9760 | tf_op jit(solution)/shard_map/ppermute | solution.py:22
  75.5 3.8 %all-to-all-start.3 = ((bf16[32,8,256]{2,1,0:T(8,128)(2,1)}), bf16[32,8,256]{2,1,0:T(8,128)(2,1)S(1)}, u32[]{:S(2)}, u32[]{:S(2)}) async-start(bf16[32,8,256]{2,1,0:T(8,128)(2,1)} %broadcast_in_dim.46), calls=%async_computation.3 | async-start | bytes 262144 | tf_op jit(solution)/shard_map/all_to_all | solution.py:31
  79.3 0.9 fusion.22
  80.6 9.0 %all-to-all-done.3 = bf16[32,8,256]{2,1,0:T(8,128)(2,1)S(1)} async-done(((bf16[32,8,256]{2,1,0:T(8,128)(2,1)}), bf16[32,8,256]{2,1,0:T(8,128)(2,1)S(1)}, u32[]{:S(2)}, u32[]{:S(2)}) %all-to-all-start.3) | async-done | bytes 131104 | tf_op jit(solution)/shard_map/all_to_all | solution.py:31
  89.7 1.2 %collective-permute-done.9 = bf16[32,8,256]{2,1,0:T(8,128)(2,1)S(1)} collective-permute-done((bf16[32,8,256]{2,1,0:T(8,128)(2,1)S(1)}, bf16[32,8,256]{2,1,0:T(8,128)(2,1)S(1)}, u32[]{:S(2)}, u32[]{:S(2)}) %collective-permute-start.9) | collective-permute-done | bytes 131104 | tf_op jit(solution)/shard_map/ppermute | solution.py:16
  91.0 2.2 %subtract_convert_fusion.3 = (bf16[8,64]{1,0:T(8,128)(2,1)S(1)}, f32[8,64]{1,0:T(8,128)S(1)}) fusion(f32[8,256]{1,0:T(8,128)S(1)} %fusion.13, bf16[8,16384]{1,0:T(8,128)(2,1)S(1)} %bitcast.92, bf16[64,16384]{1,0:T(8,128)(2,1)} %param.17), kind=kOutput, calls=%fused_computation.59 | convolution fusion | flops 16778240 | bytes 2364416 | tf_op jit(solution)/shard_map/dot_general | solution.py:158
  93.6 1.0 collective-permute-done.10
  94.9 2.4 %collective-permute-start.12 = (f32[8,48]{1,0:T(8,128)S(1)}, f32[8,48]{1,0:T(8,128)S(1)}, u32[]{:S(2)}, u32[]{:S(2)}) collective-permute-start(f32[8,48]{1,0:T(8,128)S(1)} %add.62), channel_id=1, source_target_pairs={{0,2},{1,3},{2,0},{3,1},{4,6},{5,7},{6,4},{7,5},{8,10},{9,11},{10,... | collective-permute-start | bytes 4616 | tf_op jit(solution)/shard_map/ppermute | solution.py:22
  97.3 1.4 %collective-permute-start.13 = (f32[8,48]{1,0:T(8,128)S(1)}, f32[8,48]{1,0:T(8,128)S(1)}, u32[]{:S(2)}, u32[]{:S(2)}) collective-permute-start(f32[8,48]{1,0:T(8,128)S(1)} %add.62), channel_id=1, source_target_pairs={{0,3},{1,0},{2,1},{3,2},{4,7},{5,4},{6,5},{7,6},{8,11},{9,8},{10,9... | collective-permute-start | bytes 4616 | tf_op jit(solution)/shard_map/ppermute | solution.py:22
  98.7 0.7 collective-permute-done.11
  100.0 0.9 collective-permute-done.13
  101.0 0.7 broadcast_in_dim.48
  101.7 3.8 %all-to-all-start.4 = ((f32[32,8,128]{2,1,0:T(8,128)}), f32[32,8,128]{2,1,0:T(8,128)S(1)}, u32[]{:S(2)}, u32[]{:S(2)}) async-start(f32[32,8,128]{2,1,0:T(8,128)} %broadcast_in_dim.48), calls=%async_computation.4 | async-start | bytes 262144 | tf_op jit(solution)/shard_map/all_to_all | solution.py:31
  105.6 1.1 fusion.11.head_ref
  106.7 9.2 %all-to-all-done.4.got_ref = f32[32,8,128]{2,1,0:T(8,128)S(1)} async-done(((f32[32,8,128]{2,1,0:T(8,128)}), f32[32,8,128]{2,1,0:T(8,128)S(1)}, u32[]{:S(2)}, u32[]{:S(2)}) %all-to-all-start.4) | async-done | bytes 131104 | tf_op jit(solution)/shard_map/all_to_all | solution.py:31
  115.9 1.2 %finish.1 = (f32[8,2048]{1,0:T(8,128)}, f32[8,256]{1,0:T(8,128)}, f32[8,48]{1,0:T(8,128)}) custom-call(f32[32,8,128]{2,1,0:T(8,128)S(1)} %all-to-all-done.4.got_ref, f32[8,2048]{1,0:T(8,128)S(1)} %bitcast.89, f32[8,256]{1,0:T(8,128)S(1)} %fusion.11.head_ref, f32[8,304]{1,0:T(8,128)S(1)} %add_add_fusion.top_ref, f32[48,2048]{1,0:T(8,128)S(1)} %copy-done.1, ...), custom_call_target="tpu_custom_call" | custom-call | flops 1572864 | bytes 524288 | tf_op jit(solution)/shard_map/finish/pallas_call | solution.py:71
  (57 shorter events, 7.0 us)
Async XLA Ops:
  0.6 1.7 %copy-start = (bf16[64,16384]{1,0:T(8,128)(2,1)S(1)}, bf16[64,16384]{1,0:T(8,128)(2,1)}, u32[]{:S(2)}) copy-start(bf16[64,16384]{1,0:T(8,128)(2,1)} %param.16) | copy-start | bytes 6291460
  2.3 27.9 %copy-start.1 = (f32[48,2048]{1,0:T(8,128)S(1)}, f32[48,2048]{1,0:T(8,128)}, u32[]{:S(2)}) copy-start(f32[48,2048]{1,0:T(8,128)} %sub_ref.1) | copy-start | bytes 1179652
  2.3 30.1 %copy-start.5 = (f32[8,256]{1,0:T(8,128)S(1)}, f32[8,256]{1,0:T(8,128)}, u32[]{:S(2)}) copy-start(f32[8,256]{1,0:T(8,128)} %param.12) | copy-start | bytes 24580
  2.7 29.7 %copy-start.3 = (bf16[256,4096]{1,0:T(8,128)(2,1)S(1)}, bf16[256,4096]{1,0:T(8,128)(2,1)}, u32[]{:S(2)}) copy-start(bf16[256,4096]{1,0:T(8,128)(2,1)} %param.18) | copy-start | bytes 6291460
  2.7 30.1 %copy-start.2 = (f32[48,256]{1,0:T(8,128)S(1)}, f32[48,256]{1,0:T(8,128)}, u32[]{:S(2)}) copy-start(f32[48,256]{1,0:T(8,128)} %sep_ref.1) | copy-start | bytes 147460
  2.7 1.4 %collective-permute-start = (bf16[32,8,256]{2,1,0:T(8,128)(2,1)S(1)}, bf16[32,8,256]{2,1,0:T(8,128)(2,1)S(1)}, u32[]{:S(2)}, u32[]{:S(2)}) collective-permute-start(bf16[32,8,256]{2,1,0:T(8,128)(2,1)S(1)} %fusion.7), channel_id=1, source_target_pairs={{0,4},{4,0},{1,5},{5,1},{2,6},{6,2},{3,7},{7,3},{8,12},{12,8},{9,1... | collective-permute-start | bytes 393224 | tf_op jit(solution)/shard_map/ppermute | solution.py:16
  24.5 6.2 %collective-permute-start.1 = (f32[8,256]{1,0:T(8,128)S(1)}, f32[8,256]{1,0:T(8,128)S(1)}, u32[]{:S(2)}, u32[]{:S(2)}) collective-permute-start(f32[8,256]{1,0:T(8,128)S(1)} %convert_reduce_fusion), channel_id=1, source_target_pairs={{0,1},{1,2},{2,3},{3,0},{4,5},{5,6},{6,7},{7,4},{8,9},{9,10},{10,1... | collective-permute-start | bytes 24584 | tf_op jit(solution)/shard_map/ppermute | solution.py:22
  26.0 5.2 %collective-permute-start.2 = (f32[8,256]{1,0:T(8,128)S(1)}, f32[8,256]{1,0:T(8,128)S(1)}, u32[]{:S(2)}, u32[]{:S(2)}) collective-permute-start(f32[8,256]{1,0:T(8,128)S(1)} %convert_reduce_fusion), channel_id=1, source_target_pairs={{0,2},{1,3},{2,0},{3,1},{4,6},{5,7},{6,4},{7,5},{8,10},{9,11},{10,... | collective-permute-start | bytes 24584 | tf_op jit(solution)/shard_map/ppermute | solution.py:22
  28.8 3.7 %collective-permute-start.3 = (f32[8,256]{1,0:T(8,128)S(1)}, f32[8,256]{1,0:T(8,128)S(1)}, u32[]{:S(2)}, u32[]{:S(2)}) collective-permute-start(f32[8,256]{1,0:T(8,128)S(1)} %convert_reduce_fusion), channel_id=1, source_target_pairs={{0,3},{1,0},{2,1},{3,2},{4,7},{5,4},{6,5},{7,6},{8,11},{9,8},{10,9... | collective-permute-start | bytes 24584 | tf_op jit(solution)/shard_map/ppermute | solution.py:22
  30.7 23.5 %copy-start.4 = (f32[8,2048]{1,0:T(8,128)S(1)}, f32[8,2048]{1,0:T(8,128)}, u32[]{:S(2)}) copy-start(f32[8,2048]{1,0:T(8,128)} %param.11) | copy-start | bytes 196612
  32.8 1.4 %collective-permute-start.4 = (f32[8,4096]{1,0:T(8,128)S(1)}, f32[8,4096]{1,0:T(8,128)S(1)}, u32[]{:S(2)}, u32[]{:S(2)}) collective-permute-start(f32[8,4096]{1,0:T(8,128)S(1)} %fusion.29), channel_id=1, source_target_pairs={{0,4},{4,0},{1,5},{5,1},{2,6},{6,2},{3,7},{7,3},{8,12},{12,8},{9,1... | collective-permute-start | bytes 393224 | tf_op jit(solution)/shard_map/ppermute | solution.py:16
  33.0 5.7 %collective-permute-start.5 = (f32[48,48]{1,0:T(8,128)S(1)}, f32[48,48]{1,0:T(8,128)S(1)}, u32[]{:S(2)}, u32[]{:S(2)}) collective-permute-start(f32[48,48]{1,0:T(8,128)S(1)} %fusion.2), channel_id=1, source_target_pairs={{0,4},{4,0},{1,5},{5,1},{2,6},{6,2},{3,7},{7,3},{8,12},{12,8},{9,1... | collective-permute-start | bytes 27656 | tf_op jit(solution)/shard_map/ppermute | solution.py:16
  34.8 14.7 %all-to-all-start.1 = ((f32[32,8,128]{2,1,0:T(8,128)}), f32[32,8,128]{2,1,0:T(8,128)S(1)}, u32[]{:S(2)}, u32[]{:S(2)}) async-start(f32[32,8,128]{2,1,0:T(8,128)} %add_bitcast_fusion), calls=%async_computation.1 | async-start | bytes 262144 | tf_op jit(solution)/shard_map/all_to_all | solution.py:31
  50.3 14.3 %all-to-all-start.2 = ((bf16[32,16,128]{2,1,0:T(8,128)(2,1)}), bf16[32,16,128]{2,1,0:T(8,128)(2,1)S(1)}, u32[]{:S(2)}, u32[]{:S(2)}) async-start(bf16[32,16,128]{2,1,0:T(8,128)(2,1)} %pad_maximum_fusion.1), calls=%async_computation.2 | async-start | bytes 262144 | tf_op jit(solution)/shard_map/all_to_all | solution.py:31
  66.9 6.1 %collective-permute-start.6 = (f32[8,304]{1,0:T(8,128)S(1)}, f32[8,304]{1,0:T(8,128)S(1)}, u32[]{:S(2)}, u32[]{:S(2)}) collective-permute-start(f32[8,304]{1,0:T(8,128)S(1)} %pad_maximum_fusion.2), channel_id=1, source_target_pairs={{0,1},{1,2},{2,3},{3,0},{4,5},{5,6},{6,7},{7,4},{8,9},{9,10},{10,1... | collective-permute-start | bytes 29192 | tf_op jit(solution)/shard_map/ppermute | solution.py:22
  67.2 5.8 %collective-permute-start.7 = (f32[8,304]{1,0:T(8,128)S(1)}, f32[8,304]{1,0:T(8,128)S(1)}, u32[]{:S(2)}, u32[]{:S(2)}) collective-permute-start(f32[8,304]{1,0:T(8,128)S(1)} %pad_maximum_fusion.2), channel_id=1, source_target_pairs={{0,2},{1,3},{2,0},{3,1},{4,6},{5,7},{6,4},{7,5},{8,10},{9,11},{10,... | collective-permute-start | bytes 29192 | tf_op jit(solution)/shard_map/ppermute | solution.py:22
  71.1 3.7 %collective-permute-start.8 = (f32[8,304]{1,0:T(8,128)S(1)}, f32[8,304]{1,0:T(8,128)S(1)}, u32[]{:S(2)}, u32[]{:S(2)}) collective-permute-start(f32[8,304]{1,0:T(8,128)S(1)} %pad_maximum_fusion.2), channel_id=1, source_target_pairs={{0,3},{1,0},{2,1},{3,2},{4,7},{5,4},{6,5},{7,6},{8,11},{9,8},{10,9... | collective-permute-start | bytes 29192 | tf_op jit(solution)/shard_map/ppermute | solution.py:22
  75.5 14.1 %all-to-all-start.3 = ((bf16[32,8,256]{2,1,0:T(8,128)(2,1)}), bf16[32,8,256]{2,1,0:T(8,128)(2,1)S(1)}, u32[]{:S(2)}, u32[]{:S(2)}) async-start(bf16[32,8,256]{2,1,0:T(8,128)(2,1)} %broadcast_in_dim.46), calls=%async_computation.3 | async-start | bytes 262144 | tf_op jit(solution)/shard_map/all_to_all | solution.py:31
  89.6 1.3 %collective-permute-start.9 = (bf16[32,8,256]{2,1,0:T(8,128)(2,1)S(1)}, bf16[32,8,256]{2,1,0:T(8,128)(2,1)S(1)}, u32[]{:S(2)}, u32[]{:S(2)}) collective-permute-start(bf16[32,8,256]{2,1,0:T(8,128)(2,1)S(1)} %all-to-all-done.3), channel_id=1, source_target_pairs={{0,4},{4,0},{1,5},{5,1},{2,6},{6,2},{3,7},{7,3},{8,12},{12,8},{9,1... | collective-permute-start | bytes 393224 | tf_op jit(solution)/shard_map/ppermute | solution.py:16
  93.4 1.2 %collective-permute-start.10 = (f32[8,48]{1,0:T(8,128)S(1)}, f32[8,48]{1,0:T(8,128)S(1)}, u32[]{:S(2)}, u32[]{:S(2)}) collective-permute-start(f32[8,48]{1,0:T(8,128)S(1)} %convolution_subtract_fusion), channel_id=1, source_target_pairs={{0,4},{4,0},{1,5},{5,1},{2,6},{6,2},{3,7},{7,3},{8,12},{12,8},{9,1... | collective-permute-start | bytes 4616 | tf_op jit(solution)/shard_map/ppermute | solution.py:16
  94.6 4.8 %collective-permute-start.11 = (f32[8,48]{1,0:T(8,128)S(1)}, f32[8,48]{1,0:T(8,128)S(1)}, u32[]{:S(2)}, u32[]{:S(2)}) collective-permute-start(f32[8,48]{1,0:T(8,128)S(1)} %add.62), channel_id=1, source_target_pairs={{0,1},{1,2},{2,3},{3,0},{4,5},{5,6},{6,7},{7,4},{8,9},{9,10},{10,1... | collective-permute-start | bytes 4616 | tf_op jit(solution)/shard_map/ppermute | solution.py:22
  94.9 5.1 %collective-permute-start.12 = (f32[8,48]{1,0:T(8,128)S(1)}, f32[8,48]{1,0:T(8,128)S(1)}, u32[]{:S(2)}, u32[]{:S(2)}) collective-permute-start(f32[8,48]{1,0:T(8,128)S(1)} %add.62), channel_id=1, source_target_pairs={{0,2},{1,3},{2,0},{3,1},{4,6},{5,7},{6,4},{7,5},{8,10},{9,11},{10,... | collective-permute-start | bytes 4616 | tf_op jit(solution)/shard_map/ppermute | solution.py:22
  97.3 3.6 %collective-permute-start.13 = (f32[8,48]{1,0:T(8,128)S(1)}, f32[8,48]{1,0:T(8,128)S(1)}, u32[]{:S(2)}, u32[]{:S(2)}) collective-permute-start(f32[8,48]{1,0:T(8,128)S(1)} %add.62), channel_id=1, source_target_pairs={{0,3},{1,0},{2,1},{3,2},{4,7},{5,4},{6,5},{7,6},{8,11},{9,8},{10,9... | collective-permute-start | bytes 4616 | tf_op jit(solution)/shard_map/ppermute | solution.py:22
  101.7 14.3 %all-to-all-start.4 = ((f32[32,8,128]{2,1,0:T(8,128)}), f32[32,8,128]{2,1,0:T(8,128)S(1)}, u32[]{:S(2)}, u32[]{:S(2)}) async-start(f32[32,8,128]{2,1,0:T(8,128)} %broadcast_in_dim.48), calls=%async_computation.4 | async-start | bytes 262144 | tf_op jit(solution)/shard_map/all_to_all | solution.py:31

commit v2 on v1

--- a/solution.py
+++ b/solution.py
@@ -43,6 +43,44 @@
 def from_tiles(value):
     count, rows, cols = value.shape
     return value.transpose(1, 0, 2).reshape(rows, count * cols)
+
+
+def stream(weight_hbm, buffer, done):
+    width = weight_hbm.shape[1] // done.shape[0]
+    copies = []
+    for index in range(done.shape[0]):
+        part = pl.ds(index * width, width)
+        copies.append(
+            pltpu.make_async_copy(weight_hbm.at[:, part], buffer.at[:, part], done.at[index])
+        )
+    for copy in copies:
+        copy.start()
+    return copies, width
+
+
+def lower_kernel(left_ref, weight_hbm, out_ref, buffer, done):
+    copies, width = stream(weight_hbm, buffer, done)
+    for index, copy in enumerate(copies):
+        part = slice(index * width, (index + 1) * width)
+        copy.wait()
+        out_ref[:, part] = jnp.dot(left_ref[...], buffer[:, part], preferred_element_type=F32)
+
+
+def weighted(kernel, left, weight, shape):
+    return pl.pallas_call(
+        kernel,
+        out_shape=jax.ShapeDtypeStruct(shape, F32),
+        in_specs=[
+            pl.BlockSpec(memory_space=pltpu.MemorySpace.VMEM),
+            pl.BlockSpec(memory_space=pltpu.MemorySpace.HBM),
+        ],
+        out_specs=pl.BlockSpec(memory_space=pltpu.MemorySpace.VMEM),
+        scratch_shapes=[pltpu.VMEM(weight.shape, weight.dtype), pltpu.SemaphoreType.DMA((8,))],
+        compiler_params=pltpu.CompilerParams(vmem_limit_bytes=52 << 20),
+        cost_estimate=pl.CostEstimate(
+            flops=16 * weight.size, bytes_accessed=2 * weight.size, transcendentals=0
+        ),
+    )(left, weight)
 
 
 def finish_kernel(got_ref, upper_ref, head_ref, top_ref, sub_ref, sep_ref, *outs):
@@ -137,7 +175,7 @@
     upper = jnp.where(live, upper, 0.0).reshape(vecs, rows)
     coef = lax.dot_general(upper, basis_sub, BY_LAST, precision=HIGH)
 
-    lower_part = jnp.dot(top_rhs.astype(BF16), sep_lower_inv, preferred_element_type=F32)
+    lower_part = weighted(lower_kernel, top_rhs.astype(BF16), sep_lower_inv, (vecs, group * lanes))
     lower_part = lower_part + swap_core(lower_part)
     mine = exchange(to_tiles(lower_part, group)).sum(0).astype(BF16)
     got = exchange(jnp.concatenate([spread(mine, group), gram], axis=1))

time: 119 us -> 121 us (1.017)
  Pallas kernels: 1.19 us -> 3.42 us
    pallas_call x0 -> x1, Pallas kernels: none -> 2.24 us  [weighted(): pl.pallas_call(kernel, out_shape=jax.ShapeDtypeStruct(shape, F32), in_spe...]
where the time goes in v2:
time: 121 us; the launch traced here: 119 us
  waiting for transfers between devices  48.5 us (40%)
  starting transfers between devices  30.4 us (25%)
  blocking collectives  20.2 us (17%)
  matrix products  11.3 us (9%)
  Pallas kernels  3.42 us (3%)
  local copies, waits for them, and re-layouts  1.9 us (2%)
  other arithmetic  1.87 us (2%)
  between operations  1.5 us (1%)
    all_to_all x4, waiting for transfers between devices, exchange(): return lax.all_to_all(value, ('y', 'z'), 0, 0, tiled=True)  38.7 us
    all_to_all x1, blocking collectives, exchange(): return lax.all_to_all(value, ('y', 'z'), 0, 0, tiled=True)  20.2 us
    all_to_all x4, starting transfers between devices, exchange(): return lax.all_to_all(value, ('y', 'z'), 0, 0, tiled=True)  15.4 us
    ppermute x9, starting transfers between devices, sum_front(): lax.ppermute(value, 'x', [(i, (i + step) % count) for i in range(count)])  14.1 us
    ppermute x9, waiting for transfers between devices, sum_front(): lax.ppermute(value, 'x', [(i, (i + step) % count) for i in range(count)])  5.64 us
    ppermute x5, waiting for transfers between devices, swap_core(): return lax.ppermute(value, 'c', [(0, 1), (1, 0)])  4.13 us
  transfers between devices with their start and end apart: 18, of which 14 were waited for; matrix products, arithmetic and copies ran while one was open for 5% of the time, Pallas kernels for 0%

profile of v2, /device:TPU:0, one launch (start us, length us, event | category | flops | bytes accessed | tf_op | source)
XLA Modules:
  0.0 119.1 jit_solution(12795621754739235459)
XLA Ops:
  0.6 1.2 %fusion.13 = f32[8,256]{1,0:T(8,128)S(1)} fusion(bf16[8,256,256]{2,1,0:T(8,128)(2,1)} %param.14, f32[8,2048]{1,0:T(8,128)} %param.11), kind=kOutput, calls=%fused_computation.25 | convolution fusion | flops 1048576 | bytes 143360 | tf_op jit(solution)/shard_map/dot_general | solution.py:148
  2.8 1.3 %collective-permute-done = bf16[32,8,256]{2,1,0:T(8,128)(2,1)S(1)} collective-permute-done((bf16[32,8,256]{2,1,0:T(8,128)(2,1)S(1)}, bf16[32,8,256]{2,1,0:T(8,128)(2,1)S(1)}, u32[]{:S(2)}, u32[]{:S(2)}) %collective-permute-start) | collective-permute-done | bytes 131104 | tf_op jit(solution)/shard_map/ppermute | solution.py:16
  4.2 20.2 %all_to_all.25 = bf16[32,8,256]{2,1,0:T(8,128)(2,1)S(1)} all-to-all(bf16[32,8,256]{2,1,0:T(8,128)(2,1)S(1)} %fusion.6), channel_id=1, replica_groups=mesh['y'=4,'z'=8,'c'=2,'x'=4] {'y','z'}, dimensions={0} | all-to-all | bytes 262144 | tf_op jit(solution)/shard_map/all_to_all | solution.py:31
  24.5 1.6 %collective-permute-start.1 = (f32[8,256]{1,0:T(8,128)S(1)}, f32[8,256]{1,0:T(8,128)S(1)}, u32[]{:S(2)}, u32[]{:S(2)}) collective-permute-start(f32[8,256]{1,0:T(8,128)S(1)} %convert_reduce_fusion), channel_id=1, source_target_pairs={{0,1},{1,2},{2,3},{3,0},{4,5},{5,6},{6,7},{7,4},{8,9},{9,10},{10,1... | collective-permute-start | bytes 24584 | tf_op jit(solution)/shard_map/ppermute | solution.py:22
  26.0 2.7 %collective-permute-start.2 = (f32[8,256]{1,0:T(8,128)S(1)}, f32[8,256]{1,0:T(8,128)S(1)}, u32[]{:S(2)}, u32[]{:S(2)}) collective-permute-start(f32[8,256]{1,0:T(8,128)S(1)} %convert_reduce_fusion), channel_id=1, source_target_pairs={{0,2},{1,3},{2,0},{3,1},{4,6},{5,7},{6,4},{7,5},{8,10},{9,11},{10,... | collective-permute-start | bytes 24584 | tf_op jit(solution)/shard_map/ppermute | solution.py:22
  28.8 1.4 %collective-permute-start.3 = (f32[8,256]{1,0:T(8,128)S(1)}, f32[8,256]{1,0:T(8,128)S(1)}, u32[]{:S(2)}, u32[]{:S(2)}) collective-permute-start(f32[8,256]{1,0:T(8,128)S(1)} %convert_reduce_fusion), channel_id=1, source_target_pairs={{0,3},{1,0},{2,1},{3,2},{4,7},{5,4},{6,5},{7,6},{8,11},{9,8},{10,9... | collective-permute-start | bytes 24584 | tf_op jit(solution)/shard_map/ppermute | solution.py:22
  31.2 1.2 %collective-permute-done.3 = f32[8,256]{1,0:T(8,128)S(1)} collective-permute-done((f32[8,256]{1,0:T(8,128)S(1)}, f32[8,256]{1,0:T(8,128)S(1)}, u32[]{:S(2)}, u32[]{:S(2)}) %collective-permute-start.3) | collective-permute-done | bytes 8224 | tf_op jit(solution)/shard_map/ppermute | solution.py:22
  32.4 2.2 %shard_map.130 = f32[8,4096]{1,0:T(8,128)S(1)} custom-call(bf16[8,256]{1,0:T(8,128)(2,1)S(1)} %subtract_convert_fusion.1.left_ref, bf16[256,4096]{1,0:T(8,128)(2,1)} %weight_hbm.1), custom_call_target="tpu_custom_call" | custom-call | flops 16777216 | bytes 2097152 | tf_op jit(solution)/shard_map/pallas_call | solution.py:70
  36.1 0.7 add_bitcast_fusion
  36.8 3.9 %all-to-all-start.1 = ((f32[32,8,128]{2,1,0:T(8,128)}), f32[32,8,128]{2,1,0:T(8,128)S(1)}, u32[]{:S(2)}, u32[]{:S(2)}) async-start(f32[32,8,128]{2,1,0:T(8,128)} %add_bitcast_fusion), calls=%async_computation.1 | async-start | bytes 262144 | tf_op jit(solution)/shard_map/all_to_all | solution.py:31
  40.7 10.8 %all-to-all-done.1 = f32[32,8,128]{2,1,0:T(8,128)S(1)} async-done(((f32[32,8,128]{2,1,0:T(8,128)}), f32[32,8,128]{2,1,0:T(8,128)S(1)}, u32[]{:S(2)}, u32[]{:S(2)}) %all-to-all-start.1) | async-done | bytes 131104 | tf_op jit(solution)/shard_map/all_to_all | solution.py:31
  51.6 0.7 pad_maximum_fusion.1
  52.3 3.8 %all-to-all-start.2 = ((bf16[32,16,128]{2,1,0:T(8,128)(2,1)}), bf16[32,16,128]{2,1,0:T(8,128)(2,1)S(1)}, u32[]{:S(2)}, u32[]{:S(2)}) async-start(bf16[32,16,128]{2,1,0:T(8,128)(2,1)} %pad_maximum_fusion.1), calls=%async_computation.2 | async-start | bytes 262144 | tf_op jit(solution)/shard_map/all_to_all | solution.py:31
  56.8 9.7 %all-to-all-done.2 = bf16[32,16,128]{2,1,0:T(8,128)(2,1)S(1)} async-done(((bf16[32,16,128]{2,1,0:T(8,128)(2,1)}), bf16[32,16,128]{2,1,0:T(8,128)(2,1)S(1)}, u32[]{:S(2)}, u32[]{:S(2)}) %all-to-all-start.2) | async-done | bytes 131104 | tf_op jit(solution)/shard_map/all_to_all | solution.py:31
  66.6 2.2 %fusion.21 = f32[8,256]{1,0:T(8,128)S(1)} fusion(bf16[256,4096]{1,0:T(8,128)(2,1)} %param.19, bf16[32,16,128]{2,1,0:T(8,128)(2,1)S(1)} %all-to-all-done.2), kind=kOutput, calls=%fused_computation.38 | convolution fusion | flops 16777216 | bytes 2170880 | tf_op jit(solution)/shard_map/dot_general | solution.py:185
  69.2 3.8 %collective-permute-start.7 = (f32[8,304]{1,0:T(8,128)S(1)}, f32[8,304]{1,0:T(8,128)S(1)}, u32[]{:S(2)}, u32[]{:S(2)}) collective-permute-start(f32[8,304]{1,0:T(8,128)S(1)} %pad_maximum_fusion.2), channel_id=1, source_target_pairs={{0,2},{1,3},{2,0},{3,1},{4,6},{5,7},{6,4},{7,5},{8,10},{9,11},{10,... | collective-permute-start | bytes 29192 | tf_op jit(solution)/shard_map/ppermute | solution.py:22
  73.1 1.9 %convolution_select_fusion = f32[8,8,256]{2,1,0:T(8,128)S(1)} fusion(bf16[8,256,256]{2,1,0:T(8,128)(2,1)} %param.15, bf16[8,256,256]{2,1,0:T(8,128)(2,1)} %param.14, bf16[8,8,256]{2,0,1:T(8,128)(2,1)S(1)} %bitcast.92, pred[8]{0:T(512)(128)(4,1)S(1)} %multiply_compare_fusion), kind=kOutput, calls=%fused_computation | convolution fusion | flops 16826368 | bytes 2195464 | tf_op jit(solution)/shard_map/vkr,krc->vkc/dot_general | solution.py:174
  75.0 1.7 %collective-permute-done.8 = f32[8,304]{1,0:T(8,128)S(1)} collective-permute-done((f32[8,304]{1,0:T(8,128)S(1)}, f32[8,304]{1,0:T(8,128)S(1)}, u32[]{:S(2)}, u32[]{:S(2)}) %collective-permute-start.8) | collective-permute-done | bytes 9760 | tf_op jit(solution)/shard_map/ppermute | solution.py:22
  77.4 3.8 %all-to-all-start.3 = ((bf16[32,8,256]{2,1,0:T(8,128)(2,1)}), bf16[32,8,256]{2,1,0:T(8,128)(2,1)S(1)}, u32[]{:S(2)}, u32[]{:S(2)}) async-start(bf16[32,8,256]{2,1,0:T(8,128)(2,1)} %broadcast_in_dim.46), calls=%async_computation.3 | async-start | bytes 262144 | tf_op jit(solution)/shard_map/all_to_all | solution.py:31
  81.3 0.9 fusion.22
  82.6 9.0 %all-to-all-done.3 = bf16[32,8,256]{2,1,0:T(8,128)(2,1)S(1)} async-done(((bf16[32,8,256]{2,1,0:T(8,128)(2,1)}), bf16[32,8,256]{2,1,0:T(8,128)(2,1)S(1)}, u32[]{:S(2)}, u32[]{:S(2)}) %all-to-all-start.3) | async-done | bytes 131104 | tf_op jit(solution)/shard_map/all_to_all | solution.py:31
  91.7 1.2 %collective-permute-done.9 = bf16[32,8,256]{2,1,0:T(8,128)(2,1)S(1)} collective-permute-done((bf16[32,8,256]{2,1,0:T(8,128)(2,1)S(1)}, bf16[32,8,256]{2,1,0:T(8,128)(2,1)S(1)}, u32[]{:S(2)}, u32[]{:S(2)}) %collective-permute-start.9) | collective-permute-done | bytes 131104 | tf_op jit(solution)/shard_map/ppermute | solution.py:16
  93.0 2.2 %subtract_convert_fusion.2 = (bf16[8,64]{1,0:T(8,128)(2,1)S(1)}, f32[8,64]{1,0:T(8,128)S(1)}) fusion(f32[8,256]{1,0:T(8,128)S(1)} %fusion.13, bf16[8,16384]{1,0:T(8,128)(2,1)S(1)} %bitcast.91, bf16[64,16384]{1,0:T(8,128)(2,1)} %param.17), kind=kOutput, calls=%fused_computation.58 | convolution fusion | flops 16778240 | bytes 2364416 | tf_op jit(solution)/shard_map/dot_general | solution.py:196
  95.5 1.0 collective-permute-done.10
  96.8 2.4 %collective-permute-start.12 = (f32[8,48]{1,0:T(8,128)S(1)}, f32[8,48]{1,0:T(8,128)S(1)}, u32[]{:S(2)}, u32[]{:S(2)}) collective-permute-start(f32[8,48]{1,0:T(8,128)S(1)} %add.62), channel_id=1, source_target_pairs={{0,2},{1,3},{2,0},{3,1},{4,6},{5,7},{6,4},{7,5},{8,10},{9,11},{10,... | collective-permute-start | bytes 4616 | tf_op jit(solution)/shard_map/ppermute | solution.py:22
  99.3 1.4 %collective-permute-start.13 = (f32[8,48]{1,0:T(8,128)S(1)}, f32[8,48]{1,0:T(8,128)S(1)}, u32[]{:S(2)}, u32[]{:S(2)}) collective-permute-start(f32[8,48]{1,0:T(8,128)S(1)} %add.62), channel_id=1, source_target_pairs={{0,3},{1,0},{2,1},{3,2},{4,7},{5,4},{6,5},{7,6},{8,11},{9,8},{10,9... | collective-permute-start | bytes 4616 | tf_op jit(solution)/shard_map/ppermute | solution.py:22
  100.7 0.7 collective-permute-done.11
  101.9 0.9 collective-permute-done.13
  103.6 3.9 %all-to-all-start.4 = ((f32[32,8,128]{2,1,0:T(8,128)}), f32[32,8,128]{2,1,0:T(8,128)S(1)}, u32[]{:S(2)}, u32[]{:S(2)}) async-start(f32[32,8,128]{2,1,0:T(8,128)} %broadcast_in_dim.48), calls=%async_computation.4 | async-start | bytes 262144 | tf_op jit(solution)/shard_map/all_to_all | solution.py:31
  107.5 1.1 fusion.11.head_ref
  108.6 9.2 %all-to-all-done.4.got_ref = f32[32,8,128]{2,1,0:T(8,128)S(1)} async-done(((f32[32,8,128]{2,1,0:T(8,128)}), f32[32,8,128]{2,1,0:T(8,128)S(1)}, u32[]{:S(2)}, u32[]{:S(2)}) %all-to-all-start.4) | async-done | bytes 131104 | tf_op jit(solution)/shard_map/all_to_all | solution.py:31
  117.9 1.2 finish.1
  (56 shorter events, 7.4 us)
Async XLA Ops:
  0.6 1.7 %copy-start = (bf16[64,16384]{1,0:T(8,128)(2,1)S(1)}, bf16[64,16384]{1,0:T(8,128)(2,1)}, u32[]{:S(2)}) copy-start(bf16[64,16384]{1,0:T(8,128)(2,1)} %param.16) | copy-start | bytes 6291460
  2.3 27.9 %copy-start.1 = (f32[48,2048]{1,0:T(8,128)S(1)}, f32[48,2048]{1,0:T(8,128)}, u32[]{:S(2)}) copy-start(f32[48,2048]{1,0:T(8,128)} %sub_ref.1) | copy-start | bytes 1179652
  2.3 30.1 %copy-start.4 = (f32[8,256]{1,0:T(8,128)S(1)}, f32[8,256]{1,0:T(8,128)}, u32[]{:S(2)}) copy-start(f32[8,256]{1,0:T(8,128)} %param.12) | copy-start | bytes 24580
  2.7 32.0 %copy-start.2 = (f32[48,256]{1,0:T(8,128)S(1)}, f32[48,256]{1,0:T(8,128)}, u32[]{:S(2)}) copy-start(f32[48,256]{1,0:T(8,128)} %sep_ref.1) | copy-start | bytes 147460
  2.7 1.4 %collective-permute-start = (bf16[32,8,256]{2,1,0:T(8,128)(2,1)S(1)}, bf16[32,8,256]{2,1,0:T(8,128)(2,1)S(1)}, u32[]{:S(2)}, u32[]{:S(2)}) collective-permute-start(bf16[32,8,256]{2,1,0:T(8,128)(2,1)S(1)} %fusion.7), channel_id=1, source_target_pairs={{0,4},{4,0},{1,5},{5,1},{2,6},{6,2},{3,7},{7,3},{8,12},{12,8},{9,1... | collective-permute-start | bytes 393224 | tf_op jit(solution)/shard_map/ppermute | solution.py:16
  24.5 6.2 %collective-permute-start.1 = (f32[8,256]{1,0:T(8,128)S(1)}, f32[8,256]{1,0:T(8,128)S(1)}, u32[]{:S(2)}, u32[]{:S(2)}) collective-permute-start(f32[8,256]{1,0:T(8,128)S(1)} %convert_reduce_fusion), channel_id=1, source_target_pairs={{0,1},{1,2},{2,3},{3,0},{4,5},{5,6},{6,7},{7,4},{8,9},{9,10},{10,1... | collective-permute-start | bytes 24584 | tf_op jit(solution)/shard_map/ppermute | solution.py:22
  26.0 5.2 %collective-permute-start.2 = (f32[8,256]{1,0:T(8,128)S(1)}, f32[8,256]{1,0:T(8,128)S(1)}, u32[]{:S(2)}, u32[]{:S(2)}) collective-permute-start(f32[8,256]{1,0:T(8,128)S(1)} %convert_reduce_fusion), channel_id=1, source_target_pairs={{0,2},{1,3},{2,0},{3,1},{4,6},{5,7},{6,4},{7,5},{8,10},{9,11},{10,... | collective-permute-start | bytes 24584 | tf_op jit(solution)/shard_map/ppermute | solution.py:22
  28.8 3.7 %collective-permute-start.3 = (f32[8,256]{1,0:T(8,128)S(1)}, f32[8,256]{1,0:T(8,128)S(1)}, u32[]{:S(2)}, u32[]{:S(2)}) collective-permute-start(f32[8,256]{1,0:T(8,128)S(1)} %convert_reduce_fusion), channel_id=1, source_target_pairs={{0,3},{1,0},{2,1},{3,2},{4,7},{5,4},{6,5},{7,6},{8,11},{9,8},{10,9... | collective-permute-start | bytes 24584 | tf_op jit(solution)/shard_map/ppermute | solution.py:22
  30.7 25.5 %copy-start.3 = (f32[8,2048]{1,0:T(8,128)S(1)}, f32[8,2048]{1,0:T(8,128)}, u32[]{:S(2)}) copy-start(f32[8,2048]{1,0:T(8,128)} %param.11) | copy-start | bytes 196612
  34.7 1.4 %collective-permute-start.4 = (f32[8,4096]{1,0:T(8,128)S(1)}, f32[8,4096]{1,0:T(8,128)S(1)}, u32[]{:S(2)}, u32[]{:S(2)}) collective-permute-start(f32[8,4096]{1,0:T(8,128)S(1)} %shard_map.130), channel_id=1, source_target_pairs={{0,4},{4,0},{1,5},{5,1},{2,6},{6,2},{3,7},{7,3},{8,12},{12,8},{9,1... | collective-permute-start | bytes 393224 | tf_op jit(solution)/shard_map/ppermute | solution.py:16
  35.0 5.7 %collective-permute-start.5 = (f32[48,48]{1,0:T(8,128)S(1)}, f32[48,48]{1,0:T(8,128)S(1)}, u32[]{:S(2)}, u32[]{:S(2)}) collective-permute-start(f32[48,48]{1,0:T(8,128)S(1)} %fusion.2), channel_id=1, source_target_pairs={{0,4},{4,0},{1,5},{5,1},{2,6},{6,2},{3,7},{7,3},{8,12},{12,8},{9,1... | collective-permute-start | bytes 27656 | tf_op jit(solution)/shard_map/ppermute | solution.py:16
  36.8 14.8 %all-to-all-start.1 = ((f32[32,8,128]{2,1,0:T(8,128)}), f32[32,8,128]{2,1,0:T(8,128)S(1)}, u32[]{:S(2)}, u32[]{:S(2)}) async-start(f32[32,8,128]{2,1,0:T(8,128)} %add_bitcast_fusion), calls=%async_computation.1 | async-start | bytes 262144 | tf_op jit(solution)/shard_map/all_to_all | solution.py:31
  52.3 14.3 %all-to-all-start.2 = ((bf16[32,16,128]{2,1,0:T(8,128)(2,1)}), bf16[32,16,128]{2,1,0:T(8,128)(2,1)S(1)}, u32[]{:S(2)}, u32[]{:S(2)}) async-start(bf16[32,16,128]{2,1,0:T(8,128)(2,1)} %pad_maximum_fusion.1), calls=%async_computation.2 | async-start | bytes 262144 | tf_op jit(solution)/shard_map/all_to_all | solution.py:31
  68.9 6.1 %collective-permute-start.6 = (f32[8,304]{1,0:T(8,128)S(1)}, f32[8,304]{1,0:T(8,128)S(1)}, u32[]{:S(2)}, u32[]{:S(2)}) collective-permute-start(f32[8,304]{1,0:T(8,128)S(1)} %pad_maximum_fusion.2), channel_id=1, source_target_pairs={{0,1},{1,2},{2,3},{3,0},{4,5},{5,6},{6,7},{7,4},{8,9},{9,10},{10,1... | collective-permute-start | bytes 29192 | tf_op jit(solution)/shard_map/ppermute | solution.py:22
  69.2 5.8 %collective-permute-start.7 = (f32[8,304]{1,0:T(8,128)S(1)}, f32[8,304]{1,0:T(8,128)S(1)}, u32[]{:S(2)}, u32[]{:S(2)}) collective-permute-start(f32[8,304]{1,0:T(8,128)S(1)} %pad_maximum_fusion.2), channel_id=1, source_target_pairs={{0,2},{1,3},{2,0},{3,1},{4,6},{5,7},{6,4},{7,5},{8,10},{9,11},{10,... | collective-permute-start | bytes 29192 | tf_op jit(solution)/shard_map/ppermute | solution.py:22
  73.0 3.7 %collective-permute-start.8 = (f32[8,304]{1,0:T(8,128)S(1)}, f32[8,304]{1,0:T(8,128)S(1)}, u32[]{:S(2)}, u32[]{:S(2)}) collective-permute-start(f32[8,304]{1,0:T(8,128)S(1)} %pad_maximum_fusion.2), channel_id=1, source_target_pairs={{0,3},{1,0},{2,1},{3,2},{4,7},{5,4},{6,5},{7,6},{8,11},{9,8},{10,9... | collective-permute-start | bytes 29192 | tf_op jit(solution)/shard_map/ppermute | solution.py:22
  77.4 14.1 %all-to-all-start.3 = ((bf16[32,8,256]{2,1,0:T(8,128)(2,1)}), bf16[32,8,256]{2,1,0:T(8,128)(2,1)S(1)}, u32[]{:S(2)}, u32[]{:S(2)}) async-start(bf16[32,8,256]{2,1,0:T(8,128)(2,1)} %broadcast_in_dim.46), calls=%async_computation.3 | async-start | bytes 262144 | tf_op jit(solution)/shard_map/all_to_all | solution.py:31
  91.6 1.3 %collective-permute-start.9 = (bf16[32,8,256]{2,1,0:T(8,128)(2,1)S(1)}, bf16[32,8,256]{2,1,0:T(8,128)(2,1)S(1)}, u32[]{:S(2)}, u32[]{:S(2)}) collective-permute-start(bf16[32,8,256]{2,1,0:T(8,128)(2,1)S(1)} %all-to-all-done.3), channel_id=1, source_target_pairs={{0,4},{4,0},{1,5},{5,1},{2,6},{6,2},{3,7},{7,3},{8,12},{12,8},{9,1... | collective-permute-start | bytes 393224 | tf_op jit(solution)/shard_map/ppermute | solution.py:16
  95.3 1.2 %collective-permute-start.10 = (f32[8,48]{1,0:T(8,128)S(1)}, f32[8,48]{1,0:T(8,128)S(1)}, u32[]{:S(2)}, u32[]{:S(2)}) collective-permute-start(f32[8,48]{1,0:T(8,128)S(1)} %convolution_subtract_fusion), channel_id=1, source_target_pairs={{0,4},{4,0},{1,5},{5,1},{2,6},{6,2},{3,7},{7,3},{8,12},{12,8},{9,1... | collective-permute-start | bytes 4616 | tf_op jit(solution)/shard_map/ppermute | solution.py:16
  96.5 4.8 %collective-permute-start.11 = (f32[8,48]{1,0:T(8,128)S(1)}, f32[8,48]{1,0:T(8,128)S(1)}, u32[]{:S(2)}, u32[]{:S(2)}) collective-permute-start(f32[8,48]{1,0:T(8,128)S(1)} %add.62), channel_id=1, source_target_pairs={{0,1},{1,2},{2,3},{3,0},{4,5},{5,6},{6,7},{7,4},{8,9},{9,10},{10,1... | collective-permute-start | bytes 4616 | tf_op jit(solution)/shard_map/ppermute | solution.py:22
  96.8 5.1 %collective-permute-start.12 = (f32[8,48]{1,0:T(8,128)S(1)}, f32[8,48]{1,0:T(8,128)S(1)}, u32[]{:S(2)}, u32[]{:S(2)}) collective-permute-start(f32[8,48]{1,0:T(8,128)S(1)} %add.62), channel_id=1, source_target_pairs={{0,2},{1,3},{2,0},{3,1},{4,6},{5,7},{6,4},{7,5},{8,10},{9,11},{10,... | collective-permute-start | bytes 4616 | tf_op jit(solution)/shard_map/ppermute | solution.py:22
  99.3 3.6 %collective-permute-start.13 = (f32[8,48]{1,0:T(8,128)S(1)}, f32[8,48]{1,0:T(8,128)S(1)}, u32[]{:S(2)}, u32[]{:S(2)}) collective-permute-start(f32[8,48]{1,0:T(8,128)S(1)} %add.62), channel_id=1, source_target_pairs={{0,3},{1,0},{2,1},{3,2},{4,7},{5,4},{6,5},{7,6},{8,11},{9,8},{10,9... | collective-permute-start | bytes 4616 | tf_op jit(solution)/shard_map/ppermute | solution.py:22
  103.6 14.3 %all-to-all-start.4 = ((f32[32,8,128]{2,1,0:T(8,128)}), f32[32,8,128]{2,1,0:T(8,128)S(1)}, u32[]{:S(2)}, u32[]{:S(2)}) async-start(f32[32,8,128]{2,1,0:T(8,128)} %broadcast_in_dim.48), calls=%async_computation.4 | async-start | bytes 262144 | tf_op jit(solution)/shard_map/all_to_all | solution.py:31
